TPU v7x, 32 devices: a whole 2x2x4 slice. The times are simulated.
32 devices in a mesh: seq: 16 (over z, y, x), tensor: 2 (over core).
Axes of the slice: x: 2, y: 2, z: 4, core: 2. Of those that a mesh axis runs over, the one named last changes fastest.
Arguments:
- tokens: bfloat16 [1024, 4096], P('seq', 'tensor'), may hold values from -6 to 6
- w_gate: bfloat16 [16, 4096, 4096], P('seq', None, 'tensor'), may hold values from -0.09375 to 0.09375
- w_up: bfloat16 [16, 4096, 4096], P('seq', None, 'tensor'), may hold values from -0.09375 to 0.09375
- w_down: bfloat16 [16, 4096, 4096], P('seq', None, 'tensor'), may hold values from -0.0625 to 0.0625
- routes: int32 [8, 2], replicated, may hold values from 0 to 7, all different within a row; in each aligned block of 8 rows (0 to 7, 8 to 15, ...) at most 3 rows name the same one
- gate_values: float32 [8, 2], replicated, may hold values from 0.1 to 0.9
Outputs:
- moe_out: bfloat16 [1024, 4096], P('seq', 'tensor')
Inputs may be any that keep to these rules, and one draw needn't show every extreme that they name: `routes`: the two experts of a block differ; every expert is named by some block and by at most 3 blocks, and one by exactly 3.
All inputs are finite; a program needn't handle non-finite values.
Results may differ from a plain program's by a relative error of at most 0.005.
Values may be sent and summed in bfloat16 or wider, within the bound.
No kernel may reach another device: no remote copies, remote signals or barrier semaphores. Data moves between devices by JAX's collectives and lax.ppermute only.
A program may use at most 128 MiB of HBM per device.

v0:
```python
import jax
import jax.numpy as jnp
from jax import lax
from jax.sharding import PartitionSpec as P

E = 8


def route_slots(routes, gate_values, expert, capacity):
    block_count = routes.shape[0]
    matches = routes == expert
    member = jnp.any(matches, axis=1).astype(jnp.int32)
    weight = jnp.sum(jnp.where(matches, gate_values, 0.0), axis=1)
    position = jnp.cumsum(member) - 1
    slot_ids = jnp.arange(capacity, dtype=jnp.int32)
    picked = (member[None, :] == 1) & (position[None, :] == slot_ids[:, None])
    block_ids = jnp.arange(block_count, dtype=jnp.int32)
    block_index = jnp.sum(jnp.where(picked, block_ids[None, :], 0), axis=1)
    slot_gate = jnp.sum(jnp.where(picked, weight[None, :], 0.0), axis=1)
    return (picked, block_index, slot_gate)


def per_device(tokens, w_gate, w_up, w_down, routes, gate_values):
    seq_count = lax.axis_size("seq")
    part_count = seq_count // E
    expert = lax.axis_index("seq") // part_count
    block_count = routes.shape[0]
    capacity = 3 * block_count // 8
    columns = lax.all_gather(tokens, "seq", axis=0, tiled=True)
    block_rows = columns.shape[0] // block_count
    feature_width = columns.shape[1]
    picked, block_index, slot_gate = route_slots(routes, gate_values, expert, capacity)
    chosen = columns.reshape(block_count, block_rows, feature_width)[block_index]
    chosen = chosen.reshape(capacity * block_rows, feature_width)
    gate_cols = w_gate[0]
    up_cols = w_up[0]
    full_rows = lax.all_gather(chosen, "tensor", axis=1, tiled=True)
    gate_sum = jnp.dot(full_rows, gate_cols, preferred_element_type=jnp.float32)
    up_sum = jnp.dot(full_rows, up_cols, preferred_element_type=jnp.float32)
    hidden = (jax.nn.silu(gate_sum) * up_sum).astype(jnp.bfloat16)
    quarter = lax.all_gather(hidden, "tensor", axis=1, tiled=True)
    partial_value = jnp.dot(quarter, w_down[0], preferred_element_type=jnp.float32)
    weighted = partial_value.reshape(capacity, block_rows, feature_width) * slot_gate[:, None, None]
    scattered = jnp.einsum(
        "lb,lrd->brd", picked.astype(jnp.float32), weighted, precision=lax.Precision.HIGHEST
    )
    scattered = scattered.reshape(block_count * block_rows, feature_width)
    summed = lax.psum_scatter(scattered, "seq", scatter_dimension=0, tiled=True)
    return summed.astype(jnp.bfloat16)


def solution(mesh):
    placed = (
        P("seq", "tensor"),
        P("seq", None, "tensor"),
        P("seq", None, "tensor"),
        P("seq", None, "tensor"),
        P(),
        P(),
    )
    return jax.shard_map(
        per_device, mesh=mesh, in_specs=placed, out_specs=P("seq", "tensor"), check_vma=False
    )
```

profile of v0, /device:TPU:10, one launch (start us, length us, event | category | flops | bytes accessed | tf_op | source)
XLA Modules:
  0.0 356.7 jit_solution(6207690128557403853)
XLA Ops:
  6.5 0.0 all-gather.4.cloned.1.call-start
  6.5 0.7 all-gather.4.cloned.1.call-update
  7.3 0.0 all-gather.6.cloned.1.call-start
  7.3 0.7 fusion.13
  8.0 0.2 reduce-window.8
  8.2 0.1 select_reduce_fusion.1
  8.4 78.5 %all-gather.4.cloned.1.call-done = bf16[1024,2048]{1,0:T(8,128)(2,1)} async-done(((bf16[64,2048]{1,0:T(8,128)(2,1)}), bf16[1024,2048]{1,0:T(8,128)(2,1)}) %all-gather.4.cloned.1.call-update) | async-done | bytes 4194320 | tf_op jit(solution)/shard_map/all_gather | solution.py:29
  86.8 4.1 %gather_fusion = bf16[3,128,2048]{2,1,0:T(8,128)(2,1)} fusion(bf16[8,128,2048]{2,1,0:T(8,128)(2,1)} %bitcast.32, s32[1024]{0:T(1024)S(1)} %pad_clamp_fusion), kind=kCustom, calls=%fused_computation | custom fusion | bytes 3145740 | tf_op jit(solution)/shard_map/gather | solution.py:33
  90.9 0.0 all-gather.6.cloned.1.call-update
  90.9 0.0 all-gather.8.cloned.1.call-start
  91.0 11.1 %all-gather.6.cloned.1.call-done = bf16[384,4096]{1,0:T(8,128)(2,1)} async-done(((bf16[384,2048]{1,0:T(8,128)(2,1)}), bf16[384,4096]{1,0:T(8,128)(2,1)}) %all-gather.6.cloned.1.call-update) | async-done | bytes 3145744 | tf_op jit(solution)/shard_map/all_gather | solution.py:37
  102.1 0.0 copy-start.2
  102.1 13.2 %fusion.4 = f32[384,2048]{1,0:T(8,128)S(1)} fusion(bf16[384,4096]{1,0:T(8,128)(2,1)} %all-gather.6.cloned.1.call-done, bf16[1,4096,2048]{2,1,0:T(8,128)(2,1)} %param.7), kind=kOutput, calls=%fused_computation.5 | convolution fusion | flops 6442450944 | bytes 23068672 | tf_op jit(solution)/shard_map/dot_general | solution.py:38
  115.3 0.0 copy-done.2
  115.3 0.0 copy-start
  115.3 0.0 copy-start.1
  115.3 11.3 %multiply_convert_fusion = bf16[384,2048]{1,0:T(8,128)(2,1)} fusion(f32[384,2048]{1,0:T(8,128)S(1)} %fusion.4, bf16[384,4096]{1,0:T(8,128)(2,1)S(1)} %copy-done.2, bf16[1,4096,2048]{2,1,0:T(8,128)(2,1)} %param.8), kind=kOutput, calls=%fused_computation.9 | convolution fusion | flops 6447169536 | bytes 24641536 | tf_op jit(solution)/shard_map/dot_general | solution.py:39
  126.7 0.0 all-gather.8.cloned.1.call-update
  126.7 0.0 reduce-scatter.2.cloned.1.call-start
  126.8 0.0 copy-done
  126.8 0.0 copy-done.1
  126.8 0.1 select_reduce_fusion
  126.9 13.2 %all-gather.8.cloned.1.call-done = bf16[384,4096]{1,0:T(8,128)(2,1)} async-done(((bf16[384,2048]{1,0:T(8,128)(2,1)}), bf16[384,4096]{1,0:T(8,128)(2,1)}) %all-gather.8.cloned.1.call-update) | async-done | bytes 3145744 | tf_op jit(solution)/shard_map/all_gather | solution.py:41
  140.2 11.3 %fusion = f32[3,128,2048]{2,1,0:T(8,128)S(1)} fusion(bf16[3,128,4096]{2,1,0:T(8,128)(2,1)} %bitcast.33, bf16[1,4096,2048]{2,1,0:T(8,128)(2,1)} %param.9), kind=kOutput, calls=%fused_computation.1 | convolution fusion | flops 6442450944 | bytes 23068672 | tf_op jit(solution)/shard_map/dot_general | solution.py:42
  151.5 6.7 %fusion.6 = f32[8,128,2048]{2,0,1:T(8,128)S(1)} fusion(f32[3,128,2048]{2,1,0:T(8,128)S(1)} %fusion, f32[3]{0:T(128)S(1)} %select_reduce_fusion, s32[8]{0:T(128)S(1)} %add_bitcast_fusion, pred[8]{0:T(512)(128)(4,1)S(1)} %get-tuple-element.5), kind=kOutput, calls=%fused_computation.8 | convolution fusion | flops 76283952 | bytes 11534388 | tf_op jit(solution)/shard_map/lb,lrd->brd/dot_general | solution.py:44
  158.2 8.1 %copy.7 = f32[8,128,2048]{2,1,0:T(8,128)} copy(f32[8,128,2048]{2,0,1:T(8,128)S(1)} %fusion.6) | data formatting | bytes 16777216 | tf_op jit(solution)/shard_map/lb,lrd->brd/dot_general | solution.py:44
  166.3 0.0 reduce-scatter.2.cloned.1.call-update
  166.3 182.1 %reduce-scatter.2.cloned.1.call-done = f32[64,2048]{1,0:T(8,128)} async-done(((f32[1024,2048]{1,0:T(8,128)}), f32[64,2048]{1,0:T(8,128)}) %reduce-scatter.2.cloned.1.call-update) | async-done | bytes 524304 | tf_op jit(solution)/shard_map/reduce_scatter | solution.py:48
  348.4 1.8 convert_element_type.32
  (5 shorter events, 0.1 us)
Async XLA Ops:
  6.5 80.3 %all-gather.4.cloned.1.call-start = ((), (), s32[]{:S(2)}) async-start(), calls=%async_computation.1 | async-start | bytes 4456448 | tf_op jit(solution)/shard_map/all_gather | solution.py:29
  7.3 94.8 %all-gather.6.cloned.1.call-start = ((), (), s32[]{:S(2)}) async-start(), calls=%async_computation.2 | async-start | bytes 4718592 | tf_op jit(solution)/shard_map/all_gather | solution.py:37
  90.9 49.2 %all-gather.8.cloned.1.call-start = ((), (), s32[]{:S(2)}) async-start(), calls=%async_computation.3 | async-start | bytes 4718592 | tf_op jit(solution)/shard_map/all_gather | solution.py:41
  102.1 13.2 %copy-start.2 = (bf16[384,4096]{1,0:T(8,128)(2,1)S(1)}, bf16[384,4096]{1,0:T(8,128)(2,1)}, u32[]{:S(2)}) copy-start(bf16[384,4096]{1,0:T(8,128)(2,1)} %all-gather.6.cloned.1.call-done) | copy-start | bytes 9437188
  115.3 11.5 %copy-start = (s32[8,2]{0,1:T(2,128)S(1)}, s32[8,2]{0,1:T(2,128)}, u32[]{:S(2)}) copy-start(s32[8,2]{0,1:T(2,128)} %param.10) | copy-start | bytes 196
  115.3 11.4 %copy-start.1 = (f32[8,2]{0,1:T(2,128)S(1)}, f32[8,2]{0,1:T(2,128)}, u32[]{:S(2)}) copy-start(f32[8,2]{0,1:T(2,128)} %param.11) | copy-start | bytes 196
  126.7 221.7 %reduce-scatter.2.cloned.1.call-start = ((), (), s32[]{:S(2)}) async-start(), calls=%async_computation.4 | async-start | bytes 8912896 | tf_op jit(solution)/shard_map/reduce_scatter | solution.py:48
Sparse Core Ops, SparseCore 0:
  10.1 76.6 all-gather.3
  91.0 10.9 all-gather.5
  126.8 13.2 all-gather.7
  166.4 181.9 reduce-scatter.1
where the time goes:
time: 357 us
  waiting for transfers between devices  286 us (80%)
  matrix products  42.6 us (12%)
  between operations  13.2 us (4%)
  local copies, waits for them, and re-layouts  12.2 us (3%)
    reduce_scatter x1, waiting for transfers between devices, per_device(): summed = lax.psum_scatter(scattered, 'seq', scatter_dimension=0, tiled=True)  182 us
    all_gather x1, waiting for transfers between devices, per_device(): columns = lax.all_gather(tokens, 'seq', axis=0, tiled=True)  78.5 us
    all_gather x1, waiting for transfers between devices, per_device(): quarter = lax.all_gather(hidden, 'tensor', axis=1, tiled=True)  13.2 us
    dot_general x1, matrix products, per_device(): gate_sum = jnp.dot(full_rows, gate_cols, preferred_element_type=jnp.float32)  13.2 us
    dot_general x1, matrix products, per_device(): up_sum = jnp.dot(full_rows, up_cols, preferred_element_type=jnp.float32)  11.3 us
    dot_general x1, matrix products, per_device(): jnp.dot(quarter, w_down[0], preferred_element_type=jnp.float32)  11.3 us
    all_gather x1, waiting for transfers between devices, per_device(): full_rows = lax.all_gather(chosen, 'tensor', axis=1, tiled=True)  11.1 us
    dot_general x1, local copies, waits for them, and re-layouts, per_device(): jnp.einsum('lb,lrd->brd', picked.astype(jnp.float32), weighted, precision...  8.08 us
  transfers between devices with their start and end apart: 4, of which 4 were waited for; matrix products, arithmetic and copies ran while one was open for 0% of the time, Pallas kernels for 0%

commit v1 on v0

--- a/solution.py
+++ b/solution.py
@@ -26,7 +26,9 @@
     expert = lax.axis_index("seq") // part_count
     block_count = routes.shape[0]
     capacity = 3 * block_count // 8
-    columns = lax.all_gather(tokens, "seq", axis=0, tiled=True)
+    columns = jnp.concatenate(
+        lax.all_to_all(jnp.stack([tokens] * lax.axis_size("seq")), "seq", 0, 0), axis=0
+    )
     block_rows = columns.shape[0] // block_count
     feature_width = columns.shape[1]
     picked, block_index, slot_gate = route_slots(routes, gate_values, expert, capacity)

time: 357 us -> 383 us (1.073)
  waiting for transfers between devices: 286 us -> 301 us
  starting transfers between devices: 0.12 us -> 7.45 us
    all_to_all x0 -> x1, waiting for transfers between devices: none -> 91.4 us  [per_device(): lax.all_to_all(jnp.stack([tokens] * lax.axis_size('seq')), 'seq', 0, 0)]
    all_gather x1 -> x0, waiting for transfers between devices: 78.5 us -> none  [per_device(): columns = lax.all_gather(tokens, 'seq', axis=0, tiled=True)]
    all_to_all x0 -> x1, starting transfers between devices: none -> 7.33 us  [per_device(): lax.all_to_all(jnp.stack([tokens] * lax.axis_size('seq')), 'seq', 0, 0)]
where the time goes in v1:
time: 383 us; the launch traced here: 382 us
  waiting for transfers between devices  301 us (79%)
  matrix products  42.6 us (11%)
  local copies, waits for them, and re-layouts  15.6 us (4%)
  between operations  13.2 us (3%)
  starting transfers between devices  7.45 us (2%)
    reduce_scatter x1, waiting for transfers between devices, per_device(): summed = lax.psum_scatter(scattered, 'seq', scatter_dimension=0, tiled=True)  182 us
    all_to_all x1, waiting for transfers between devices, per_device(): lax.all_to_all(jnp.stack([tokens] * lax.axis_size('seq')), 'seq', 0, 0)  91.4 us
    all_gather x1, waiting for transfers between devices, per_device(): full_rows = lax.all_gather(chosen, 'tensor', axis=1, tiled=True)  14.5 us
    all_gather x1, waiting for transfers between devices, per_device(): quarter = lax.all_gather(hidden, 'tensor', axis=1, tiled=True)  13.2 us
    dot_general x1, matrix products, per_device(): gate_sum = jnp.dot(full_rows, gate_cols, preferred_element_type=jnp.float32)  13.2 us
    dot_general x1, matrix products, per_device(): up_sum = jnp.dot(full_rows, up_cols, preferred_element_type=jnp.float32)  11.4 us
    dot_general x1, matrix products, per_device(): jnp.dot(quarter, w_down[0], preferred_element_type=jnp.float32)  11.3 us
    dot_general x1, local copies, waits for them, and re-layouts, per_device(): jnp.einsum('lb,lrd->brd', picked.astype(jnp.float32), weighted, precision...  8.08 us
  transfers between devices with their start and end apart: 4, of which 4 were waited for; matrix products, arithmetic and copies ran while one was open for 0% of the time, Pallas kernels for 0%

profile of v1, /device:TPU:10, one launch (start us, length us, event | category | flops | bytes accessed | tf_op | source)
XLA Modules:
  0.0 382.4 jit_solution(5776492369834108686)
XLA Ops:
  6.5 3.4 stack.2
  10.0 0.0 copy-start
  10.0 7.3 %all-to-all-start = ((bf16[16,64,2048]{2,1,0:T(8,128)(2,1)}), bf16[16,64,2048]{2,1,0:T(8,128)(2,1)}, u32[]{:S(2)}, u32[]{:S(2)}) async-start(bf16[16,64,2048]{2,1,0:T(8,128)(2,1)} %stack.2), calls=%async_computation | async-start | bytes 8388608 | tf_op jit(solution)/shard_map/all_to_all | solution.py:30
  17.3 0.0 all-gather.3.cloned.1.call-start
  17.4 0.0 copy-done
  17.4 0.2 reduce-window.8
  17.6 0.1 select_reduce_fusion.1
  17.7 91.4 %all-to-all-done = bf16[16,64,2048]{2,1,0:T(8,128)(2,1)} async-done(((bf16[16,64,2048]{2,1,0:T(8,128)(2,1)}), bf16[16,64,2048]{2,1,0:T(8,128)(2,1)}, u32[]{:S(2)}, u32[]{:S(2)}) %all-to-all-start) | async-done | bytes 4194336 | tf_op jit(solution)/shard_map/all_to_all | solution.py:30
  109.1 4.1 %gather_fusion = bf16[3,128,2048]{2,1,0:T(8,128)(2,1)} fusion(bf16[8,128,2048]{2,1,0:T(8,128)(2,1)} %bitcast.3, s32[1024]{0:T(1024)S(1)} %pad_clamp_fusion), kind=kCustom, calls=%fused_computation | custom fusion | bytes 3145740 | tf_op jit(solution)/shard_map/gather | solution.py:35
  113.1 0.0 all-gather.3.cloned.1.call-update
  113.2 0.0 all-gather.5.cloned.1.call-start
  113.2 14.5 %all-gather.3.cloned.1.call-done = bf16[384,4096]{1,0:T(8,128)(2,1)} async-done(((bf16[384,2048]{1,0:T(8,128)(2,1)}), bf16[384,4096]{1,0:T(8,128)(2,1)}) %all-gather.3.cloned.1.call-update) | async-done | bytes 3145744 | tf_op jit(solution)/shard_map/all_gather | solution.py:39
  127.8 0.0 copy-start.2
  127.8 13.2 %fusion.4 = f32[384,2048]{1,0:T(8,128)S(1)} fusion(bf16[384,4096]{1,0:T(8,128)(2,1)} %all-gather.3.cloned.1.call-done, bf16[1,4096,2048]{2,1,0:T(8,128)(2,1)} %param.7), kind=kOutput, calls=%fused_computation.5 | convolution fusion | flops 6442450944 | bytes 23068672 | tf_op jit(solution)/shard_map/dot_general | solution.py:40
  141.0 0.0 copy-done.2
  141.0 0.0 copy-start.1
  141.0 11.4 %multiply_convert_fusion = bf16[384,2048]{1,0:T(8,128)(2,1)} fusion(f32[384,2048]{1,0:T(8,128)S(1)} %fusion.4, bf16[384,4096]{1,0:T(8,128)(2,1)S(1)} %copy-done.2, bf16[1,4096,2048]{2,1,0:T(8,128)(2,1)} %param.8), kind=kOutput, calls=%fused_computation.9 | convolution fusion | flops 6447169536 | bytes 24641536 | tf_op jit(solution)/shard_map/dot_general | solution.py:41
  152.4 0.0 all-gather.5.cloned.1.call-update
  152.4 0.0 reduce-scatter.2.cloned.1.call-start
  152.4 0.0 copy-done.1
  152.5 0.1 select_reduce_fusion
  152.6 13.2 %all-gather.5.cloned.1.call-done = bf16[384,4096]{1,0:T(8,128)(2,1)} async-done(((bf16[384,2048]{1,0:T(8,128)(2,1)}), bf16[384,4096]{1,0:T(8,128)(2,1)}) %all-gather.5.cloned.1.call-update) | async-done | bytes 3145744 | tf_op jit(solution)/shard_map/all_gather | solution.py:43
  165.8 11.3 %fusion = f32[3,128,2048]{2,1,0:T(8,128)S(1)} fusion(bf16[3,128,4096]{2,1,0:T(8,128)(2,1)} %bitcast.32, bf16[1,4096,2048]{2,1,0:T(8,128)(2,1)} %param.9), kind=kOutput, calls=%fused_computation.1 | convolution fusion | flops 6442450944 | bytes 23068672 | tf_op jit(solution)/shard_map/dot_general | solution.py:44
  177.2 6.7 %fusion.6 = f32[8,128,2048]{2,0,1:T(8,128)S(1)} fusion(f32[3,128,2048]{2,1,0:T(8,128)S(1)} %fusion, f32[3]{0:T(128)S(1)} %select_reduce_fusion, s32[8]{0:T(128)S(1)} %add_bitcast_fusion, pred[8]{0:T(512)(128)(4,1)S(1)} %get-tuple-element.5), kind=kOutput, calls=%fused_computation.8 | convolution fusion | flops 76283952 | bytes 11534388 | tf_op jit(solution)/shard_map/lb,lrd->brd/dot_general | solution.py:46
  183.9 8.1 %copy.7 = f32[8,128,2048]{2,1,0:T(8,128)} copy(f32[8,128,2048]{2,0,1:T(8,128)S(1)} %fusion.6) | data formatting | bytes 16777216 | tf_op jit(solution)/shard_map/lb,lrd->brd/dot_general | solution.py:46
  192.0 0.0 reduce-scatter.2.cloned.1.call-update
  192.0 182.1 %reduce-scatter.2.cloned.1.call-done = f32[64,2048]{1,0:T(8,128)} async-done(((f32[1024,2048]{1,0:T(8,128)}), f32[64,2048]{1,0:T(8,128)}) %reduce-scatter.2.cloned.1.call-update) | async-done | bytes 524304 | tf_op jit(solution)/shard_map/reduce_scatter | solution.py:50
  374.1 1.8 convert_element_type.32
  (6 shorter events, 0.1 us)
Async XLA Ops:
  10.0 7.4 %copy-start = (s32[8,2]{0,1:T(2,128)S(1)}, s32[8,2]{0,1:T(2,128)}, u32[]{:S(2)}) copy-start(s32[8,2]{0,1:T(2,128)} %param.10) | copy-start | bytes 196
  10.0 99.1 %all-to-all-start = ((bf16[16,64,2048]{2,1,0:T(8,128)(2,1)}), bf16[16,64,2048]{2,1,0:T(8,128)(2,1)}, u32[]{:S(2)}, u32[]{:S(2)}) async-start(bf16[16,64,2048]{2,1,0:T(8,128)(2,1)} %stack.2), calls=%async_computation | async-start | bytes 8388608 | tf_op jit(solution)/shard_map/all_to_all | solution.py:30
  17.3 110.5 %all-gather.3.cloned.1.call-start = ((), (), s32[]{:S(2)}) async-start(), calls=%async_computation.2 | async-start | bytes 4718592 | tf_op jit(solution)/shard_map/all_gather | solution.py:39
  113.2 52.7 %all-gather.5.cloned.1.call-start = ((), (), s32[]{:S(2)}) async-start(), calls=%async_computation.3 | async-start | bytes 4718592 | tf_op jit(solution)/shard_map/all_gather | solution.py:43
  127.8 13.2 %copy-start.2 = (bf16[384,4096]{1,0:T(8,128)(2,1)S(1)}, bf16[384,4096]{1,0:T(8,128)(2,1)}, u32[]{:S(2)}) copy-start(bf16[384,4096]{1,0:T(8,128)(2,1)} %all-gather.3.cloned.1.call-done) | copy-start | bytes 9437188
  141.0 11.4 %copy-start.1 = (f32[8,2]{0,1:T(2,128)S(1)}, f32[8,2]{0,1:T(2,128)}, u32[]{:S(2)}) copy-start(f32[8,2]{0,1:T(2,128)} %param.11) | copy-start | bytes 196
  152.4 221.7 %reduce-scatter.2.cloned.1.call-start = ((), (), s32[]{:S(2)}) async-start(), calls=%async_computation.4 | async-start | bytes 8912896 | tf_op jit(solution)/shard_map/reduce_scatter | solution.py:50
Sparse Core Ops, SparseCore 0:
  113.3 14.4 all-gather.2
  152.5 13.2 all-gather.4
  192.1 181.9 reduce-scatter.1
